TPU v7x, 32 devices: a whole 2x2x4 slice. The times are simulated.
32 devices in a mesh: ctx: 8 (over z, x), tp: 4 (over y, core).
Axes of the slice: x: 2, y: 2, z: 4, core: 2. Of those that a mesh axis runs over, the one named last changes fastest.
Arguments:
- q_nope: bfloat16 [8, 128, 128], P('ctx', 'tp'), may hold values from -6 to 6
- q_rope: bfloat16 [8, 128, 64], P('ctx', 'tp'), may hold values from -256 to 256
- w_uk: bfloat16 [128, 128, 512], P('tp'), may hold values from -0.5 to 0.5
- w_uv: bfloat16 [128, 512, 128], P('tp'), may hold values from -3 to 3
- w_out: bfloat16 [16384, 7168], P('tp', 'ctx'), may hold values from -0.046875 to 0.046875
- prefix_cache: bfloat16 [32768, 576], P('ctx'), may hold values from -6 to 6
- block_table: int32 [512], P('ctx'), may hold values from 0 to 511, each once
- prefix_len: int32 [8], replicated, may hold values from 8192 to 32768
- suffix_cache: bfloat16 [8, 256, 576], P('ctx'), may hold values from -12 to 12
- suffix_len: int32 [8], P('ctx'), may hold values from 2 to 256
Outputs:
- layer_out: bfloat16 [8, 7168], P('tp', 'ctx')
Inputs may be any that keep to these rules, and one draw needn't show every extreme that they name: A permutation: slots b * 64 to b * 64 + 63 of prefix_cache hold prefix positions block_table[b] * 64 onwards.
All inputs are finite; a program needn't handle non-finite values.
Results may differ from a plain program's by a relative error of at most 0.0078.
Values may be sent and summed in bfloat16 or wider, within the bound.
A program may use at most 64 MiB of HBM per device.

v0:
```python
import jax
import jax.numpy as jnp
from jax import lax
from jax.sharding import PartitionSpec as P

LAT = 512
ROPE = 64
NOPE = 128
BLOCK = 64
masked_value = -1e30


def partial_stats(scores, visible, values, pattern):
    row_peak = jnp.max(jnp.where(visible, scores, masked_value), axis=2)
    weights = jnp.where(visible, jnp.exp(scores - row_peak[:, :, None]), 0.0).astype(jnp.bfloat16)
    row_mass = jnp.sum(weights, axis=2, dtype=jnp.float32)
    row_weighted = jnp.einsum(pattern, weights, values, preferred_element_type=jnp.float32)
    return (row_peak, row_mass, row_weighted)


def value_project(latent, value_weight):
    return jnp.einsum("rhc,hcv->rhv", latent, value_weight, precision=lax.Precision.HIGHEST)


def on_device(
    q_nope,
    q_rope,
    w_uk,
    w_uv,
    w_out,
    prefix_cache,
    block_table,
    prefix_len,
    suffix_cache,
    suffix_len,
):
    softmax_scale = (NOPE + ROPE) ** (-0.5)
    q_latent = jnp.einsum("rhn,hnc->rhc", q_nope, w_uk, preferred_element_type=jnp.float32).astype(
        jnp.bfloat16
    )
    own_queries = jnp.concatenate([q_latent, q_rope], axis=2)
    all_queries = lax.all_gather(own_queries, "ctx", axis=0, tiled=True)
    ctx_count = lax.axis_size("ctx")
    own_count = own_queries.shape[0]
    value_weight = w_uv.astype(jnp.float32)
    positions = (
        block_table[:, None] * BLOCK + jnp.arange(BLOCK, dtype=jnp.int32)[None, :]
    ).reshape(-1)
    visible = (positions[None, :] < prefix_len[:, None])[:, None, :]
    scores = (
        jnp.einsum("rhc,tc->rht", all_queries, prefix_cache, preferred_element_type=jnp.float32)
        * softmax_scale
    )
    row_peak, row_mass, row_weighted = partial_stats(
        scores, visible, prefix_cache[:, :LAT], "rht,tc->rhc"
    )
    suffix_scores = (
        jnp.einsum("rhc,rtc->rht", own_queries, suffix_cache, preferred_element_type=jnp.float32)
        * softmax_scale
    )
    suffix_slots = jnp.arange(suffix_cache.shape[1], dtype=jnp.int32)
    suffix_visible = (suffix_slots[None, :] < suffix_len[:, None])[:, None, :]
    tail_peak, tail_mass, tail_weighted = partial_stats(
        suffix_scores, suffix_visible, suffix_cache[:, :, :LAT], "rht,rtc->rhc"
    )

    def by_owner(values):
        return values.reshape((ctx_count, own_count) + values.shape[1:])

    got_peak, got_mass, got_weighted = (
        lax.all_to_all(by_owner(row_peak), "ctx", split_axis=0, concat_axis=0, tiled=True),
        lax.all_to_all(by_owner(row_mass), "ctx", split_axis=0, concat_axis=0, tiled=True),
        lax.all_to_all(by_owner(row_weighted), "ctx", split_axis=0, concat_axis=0, tiled=True),
    )
    highest = jnp.maximum(jnp.max(got_peak, axis=0), tail_peak)
    factors = jnp.exp(got_peak - highest[None])
    tail_factor = jnp.exp(tail_peak - highest)
    total_mass = jnp.sum(factors * got_mass, axis=0) + tail_factor * tail_mass
    total_weighted = (
        jnp.sum(factors[..., None] * got_weighted, axis=0) + tail_factor[:, :, None] * tail_weighted
    )
    head_values = value_project(total_weighted / total_mass[:, :, None], value_weight).astype(
        jnp.bfloat16
    )
    flat_values = head_values.reshape(own_count, -1)
    every_value = lax.all_gather(flat_values, "ctx", axis=0, tiled=True)
    return lax.psum_scatter(
        jnp.dot(every_value, w_out, preferred_element_type=jnp.float32),
        "tp",
        scatter_dimension=0,
        tiled=True,
    ).astype(jnp.bfloat16)


def solution(mesh):
    placed = (
        P("ctx", "tp", None),
        P("ctx", "tp", None),
        P("tp", None, None),
        P("tp", None, None),
        P("tp", "ctx"),
        P("ctx", None),
        P("ctx"),
        P(),
        P("ctx", None, None),
        P("ctx"),
    )
    return jax.shard_map(
        on_device, mesh=mesh, in_specs=placed, out_specs=P("tp", "ctx"), check_vma=False
    )
```

profile of v0, /device:TPU:0, one launch (start us, length us, event | category | flops | bytes accessed | tf_op | source)
XLA Modules:
  0.0 129.5 jit_solution(10840114998855403633)
XLA Ops:
  0.0 0.0 copy-start
  0.0 0.0 copy-start.3
  0.0 0.0 copy-start.4
  0.0 0.7 broadcast_multiply_fusion
  0.7 0.1 iota_add_fusion
  0.8 0.1 add.38
  0.9 0.0 copy-done
  0.9 0.0 copy-start.5
  0.9 3.0 %fusion.20 = bf16[32,1,512]{2,1,0:T(2,128)(2,1)S(1)} fusion(bf16[32,128,512]{2,1,0:T(8,128)(2,1)} %param.12, bf16[32,128,1]{1,0,2:T(8,128)(2,1)S(1)} %bitcast.55), kind=kOutput, calls=%fused_computation.32 | convolution fusion | flops 4194304 | bytes 4235264 | tf_op jit(solution)/shard_map/rhn,hnc->rhc/dot_general | solution.py:38
  3.9 0.0 copy-done.3
  3.9 32.7 %all_gather.6 = bf16[8,32,576]{2,1,0:T(8,128)(2,1)S(1)} all-gather(bf16[1,32,576]{2,1,0:T(8,128)(2,1)S(1)} %pad_maximum_fusion), channel_id=1, replica_groups=mesh['ctx'=8,'tp'=4] {'ctx'}, dimensions={0}, use_global_device_ids=true | all-gather | bytes 331776 | tf_op jit(solution)/shard_map/all_gather | solution.py:42
  36.6 0.0 copy-done.4
  36.6 0.1 broadcast_compare_fusion
  36.7 0.0 copy-done.5
  36.7 2.7 %select_reduce_fusion = (f32[8,32]{1,0:T(8,128)}, f32[8,32,4096]{2,1,0:T(8,128)S(1)}) fusion(pred[8,4096]{1,0:T(8,128)(4,1)S(1)} %broadcast_compare_fusion, bf16[8,32,576]{2,1,0:T(8,128)(2,1)S(1)} %all_gather.6, bf16[4096,576]{0,1:T(8,128)(2,1)S(1)} %copy-done.5), kind=kOutput, calls=%fused_computation.7 | convolution fusion | flops 1211105024 | bytes 9241600 | tf_op jit(solution)/shard_map/rhc,tc->rht/dot_general | solution.py:51
  39.4 0.0 copy-start.1
  39.4 1.9 %copy-done.1 = f32[8,32,4096]{2,1,0:T(8,128)} copy-done((f32[8,32,4096]{2,1,0:T(8,128)}, f32[8,32,4096]{2,1,0:T(8,128)S(1)}, u32[]{:S(2)}) %copy-start.1) | copy-done | bytes 4194328
  41.3 1.7 %convert_reduce_fusion = f32[8,32]{1,0:T(8,128)S(1)} fusion(f32[8,32,4096]{2,1,0:T(8,128)S(1)} %get-tuple-element.10, f32[8,32]{1,0:T(8,128)} %get-tuple-element.9, pred[8,4096]{1,0:T(8,128)(4,1)S(1)} %broadcast_compare_fusion), kind=kLoop, calls=%fused_computation.4 | loop fusion | flops 5242624 | bytes 4229120 | tf_op jit(solution)/shard_map/reduce_sum | solution.py:16
  43.0 11.8 %all_to_all.15 = f32[8,1,32]{2,1,0:T(1,128)S(1)} all-to-all(f32[8,1,32]{2,1,0:T(1,128)S(1)} %bitcast.60), channel_id=1, replica_groups=mesh['ctx'=8,'tp'=4] {'ctx'}, dimensions={0} | all-to-all | bytes 2048 | tf_op jit(solution)/shard_map/all_to_all | solution.py:72
  54.9 3.2 %all-to-all-start = ((f32[8,1,32]{2,1,0:T(1,128)}), f32[8,1,32]{2,1,0:T(1,128)S(1)}, u32[]{:S(2)}, u32[]{:S(2)}) async-start(f32[8,1,32]{2,1,0:T(1,128)} %bitcast.5), calls=%async_computation | async-start | bytes 8192 | tf_op jit(solution)/shard_map/all_to_all | solution.py:71
  58.1 0.0 copy-start.6
  58.1 0.0 copy-start.2
  58.1 5.6 %fusion.4 = f32[8,1,32,512]{3,2,1,0:T(8,128)} fusion(bf16[4096,576]{0,1:T(8,128)(2,1)} %param.15, f32[8,32,4096]{2,1,0:T(8,128)} %copy-done.1, f32[8,32]{1,0:T(8,128)} %get-tuple-element.9, pred[8,4096]{1,0:T(8,128)(4,1)S(1)} %broadcast_compare_fusion), kind=kOutput, calls=%fused_computation.8 | convolution fusion | flops 1076887552 | bytes 8949760 | tf_op jit(solution)/shard_map/rht,tc->rhc/dot_general | solution.py:17
  63.7 0.8 all-to-all-done
  64.5 5.1 %all-to-all-start.1 = ((f32[8,1,32,512]{3,2,1,0:T(8,128)}), f32[8,1,32,512]{3,2,1,0:T(8,128)S(1)}, u32[]{:S(2)}, u32[]{:S(2)}) async-start(f32[8,1,32,512]{3,2,1,0:T(8,128)} %fusion.4), calls=%async_computation.1 | async-start | bytes 1048576 | tf_op jit(solution)/shard_map/all_to_all | solution.py:73
  70.3 0.0 copy-done.6
  70.3 0.7 dynamic-slice
  71.7 0.0 copy-done.2
  71.7 0.3 select_reduce_fusion.1
  72.0 0.2 convert_reduce_fusion.1
  72.2 7.8 %all-to-all-done.1 = f32[8,1,32,512]{3,2,1,0:T(8,128)S(1)} async-done(((f32[8,1,32,512]{3,2,1,0:T(8,128)}), f32[8,1,32,512]{3,2,1,0:T(8,128)S(1)}, u32[]{:S(2)}, u32[]{:S(2)}) %all-to-all-start.1) | async-done | bytes 524320 | tf_op jit(solution)/shard_map/all_to_all | solution.py:73
  80.0 0.1 multiply_reduce_fusion
  80.1 0.2 fusion.9
  80.3 3.5 %fusion.16 = f32[32,1,128]{2,1,0:T(1,128)S(1)} fusion(bf16[32,512,128]{2,1,0:T(8,128)(2,1)} %param.13, f32[32,512,1]{1,0,2:T(8,128)S(1)} %fusion.9), kind=kOutput, calls=%fused_computation.22 | convolution fusion | flops 25165824 | bytes 4276224 | tf_op jit(solution)/shard_map/rhc,hcv->rhv/dot_general | solution.py:22
  83.9 30.5 %all-gather = bf16[8,1,4096]{2,1,0:T(2,128)(2,1)S(1)} all-gather(bf16[1,1,4096]{2,1,0:T(2,128)(2,1)S(1)} %reshape.166), channel_id=1, replica_groups=mesh['ctx'=8,'tp'=4] {'ctx'}, dimensions={0}, use_global_device_ids=true | all-gather | bytes 73728 | tf_op jit(solution)/shard_map/all_gather | solution.py:86
  114.4 4.1 %fusion.13 = f32[8,896]{1,0:T(8,128)S(1)} fusion(bf16[4096,896]{1,0:T(8,128)(2,1)} %param.14, bf16[8,1,4096]{2,1,0:T(2,128)(2,1)S(1)} %all-gather), kind=kOutput, calls=%fused_computation.18 | convolution fusion | flops 58720256 | bytes 7434240 | tf_op jit(solution)/shard_map/dot_general | solution.py:88
  118.6 10.3 %all-reduce = bf16[8,896]{1,0:T(8,128)(2,1)S(1)} all-reduce(f32[8,896]{1,0:T(8,128)S(1)} %fusion.13), channel_id=2, replica_groups=mesh['ctx'=8,'tp'=4] {'tp'}, use_global_device_ids=true, to_apply=%region_7.8.clone | all-reduce | flops 7168 | bytes 43008
  128.9 0.6 dynamic-slice_convert_fusion
  (9 shorter events, 0.1 us)
Async XLA Ops:
  0.0 0.9 copy-start
  0.0 3.9 %copy-start.3 = (bf16[1,32,64]{2,1,0:T(8,128)(2,1)S(1)}, bf16[1,32,64]{2,1,0:T(8,128)(2,1)}, u32[]{:S(2)}) copy-start(bf16[1,32,64]{2,1,0:T(8,128)(2,1)} %param.11) | copy-start | bytes 12292
  0.0 36.6 %copy-start.4 = (s32[8]{0:T(128)S(1)}, s32[8]{0:T(128)}, u32[]{:S(2)}) copy-start(s32[8]{0:T(128)} %param.17) | copy-start | bytes 100
  0.9 35.8 %copy-start.5 = (bf16[4096,576]{0,1:T(8,128)(2,1)S(1)}, bf16[4096,576]{0,1:T(8,128)(2,1)}, u32[]{:S(2)}) copy-start(bf16[4096,576]{0,1:T(8,128)(2,1)} %param.15) | copy-start | bytes 14155780
  39.4 1.9 %copy-start.1 = (f32[8,32,4096]{2,1,0:T(8,128)}, f32[8,32,4096]{2,1,0:T(8,128)S(1)}, u32[]{:S(2)}) copy-start(f32[8,32,4096]{2,1,0:T(8,128)S(1)} %get-tuple-element.10) | copy-start | bytes 12582916
  54.9 9.7 %all-to-all-start = ((f32[8,1,32]{2,1,0:T(1,128)}), f32[8,1,32]{2,1,0:T(1,128)S(1)}, u32[]{:S(2)}, u32[]{:S(2)}) async-start(f32[8,1,32]{2,1,0:T(1,128)} %bitcast.5), calls=%async_computation | async-start | bytes 8192 | tf_op jit(solution)/shard_map/all_to_all | solution.py:71
  58.1 12.2 %copy-start.6 = (u32[32]{0:T(128)S(1)}, u32[32]{0:T(128)}, u32[]{:S(2)}) copy-start(u32[32]{0:T(128)} %constant.17) | copy-start | bytes 388
  58.1 13.6 %copy-start.2 = (bf16[1,256,576]{1,2,0:T(8,128)(2,1)S(1)}, bf16[1,256,576]{1,2,0:T(8,128)(2,1)}, u32[]{:S(2)}) copy-start(bf16[1,256,576]{1,2,0:T(8,128)(2,1)} %param.18) | copy-start | bytes 884740
  64.5 15.5 %all-to-all-start.1 = ((f32[8,1,32,512]{3,2,1,0:T(8,128)}), f32[8,1,32,512]{3,2,1,0:T(8,128)S(1)}, u32[]{:S(2)}, u32[]{:S(2)}) async-start(f32[8,1,32,512]{3,2,1,0:T(8,128)} %fusion.4), calls=%async_computation.1 | async-start | bytes 1048576 | tf_op jit(solution)/shard_map/all_to_all | solution.py:73
where the time goes:
time: 130 us; the launch traced here: 129 us
  blocking collectives  85.4 us (66%)
  matrix products  19.4 us (15%)
  waiting for transfers between devices  8.58 us (7%)
  starting transfers between devices  8.34 us (6%)
  local copies, waits for them, and re-layouts  3.31 us (3%)
  other arithmetic  3 us (2%)
  between operations  1.49 us (1%)
    all_gather x1, blocking collectives, on_device(): all_queries = lax.all_gather(own_queries, 'ctx', axis=0, tiled=True)  32.7 us
    all_gather x1, blocking collectives, on_device(): every_value = lax.all_gather(flat_values, 'ctx', axis=0, tiled=True)  30.5 us
    all_to_all x1, blocking collectives, on_device(): lax.all_to_all(by_owner(row_mass), 'ctx', split_axis=0, concat_axis=0, ti...  11.8 us
    unnamed x1, blocking collectives  10.3 us
    all_to_all x1, waiting for transfers between devices, on_device(): lax.all_to_all(by_owner(row_weighted), 'ctx', split_axis=0, concat_axis=0...  7.78 us
    dot_general x2, matrix products, partial_stats(): jnp.einsum(pattern, weights, values, preferred_element_type=jnp.float32)  5.81 us
    all_to_all x1, starting transfers between devices, on_device(): lax.all_to_all(by_owner(row_weighted), 'ctx', split_axis=0, concat_axis=0...  5.12 us
    dot_general x1, matrix products, on_device(): jnp.dot(every_value, w_out, preferred_element_type=jnp.float32)  4.14 us
  transfers between devices with their start and end apart: 2, of which 2 were waited for; matrix products, arithmetic and copies ran while one was open for 5% of the time, Pallas kernels for 0%

commit v1 on v0

--- a/solution.py
+++ b/solution.py
@@ -8,6 +8,21 @@
 NOPE = 128
 BLOCK = 64
 masked_value = -1e30
+
+
+def on_each_block(shard, axis, dim, make, out_dim):
+    ways, here, step = (lax.axis_size(axis), lax.axis_index(axis), shard.shape[dim])
+    results = []
+    for far in range(ways):
+        arriving = (
+            lax.ppermute(shard, axis, [(d, (d + 1) % ways) for d in range(ways)])
+            if far + 1 < ways
+            else shard
+        )
+        results.append(make(shard, (here - far) % ways * step))
+        shard = arriving
+    line = jnp.concatenate(results[::-1], axis=out_dim)
+    return jnp.roll(line, (here + 1) * results[0].shape[out_dim], axis=out_dim)
 
 
 def partial_stats(scores, visible, values, pattern):
@@ -39,7 +54,6 @@
         jnp.bfloat16
     )
     own_queries = jnp.concatenate([q_latent, q_rope], axis=2)
-    all_queries = lax.all_gather(own_queries, "ctx", axis=0, tiled=True)
     ctx_count = lax.axis_size("ctx")
     own_count = own_queries.shape[0]
     value_weight = w_uv.astype(jnp.float32)
@@ -48,7 +62,15 @@
     ).reshape(-1)
     visible = (positions[None, :] < prefix_len[:, None])[:, None, :]
     scores = (
-        jnp.einsum("rhc,tc->rht", all_queries, prefix_cache, preferred_element_type=jnp.float32)
+        on_each_block(
+            own_queries,
+            "ctx",
+            0,
+            lambda own_block, start: jnp.einsum(
+                "rhc,tc->rht", own_block, prefix_cache, preferred_element_type=jnp.float32
+            ),
+            0,
+        )
         * softmax_scale
     )
     row_peak, row_mass, row_weighted = partial_stats(

time: 130 us -> 152 us (1.17)
  waiting for transfers between devices: 8.58 us -> 52.7 us
  blocking collectives: 85.4 us -> 49.7 us
  matrix products: 19.4 us -> 26.4 us
  other arithmetic: 3 us -> 6.28 us
  starting transfers between devices: 8.34 us -> 11.4 us
    ppermute x0 -> x7, waiting for transfers between devices: none -> 43.9 us  [on_each_block(): lax.ppermute(shard, axis, [(d, (d + 1) % ways) for d in range(ways)])]
    all_gather x1 -> x0, blocking collectives: 32.7 us -> none  [on_device(): all_queries = lax.all_gather(own_queries, 'ctx', axis=0, tiled=True)]
    dot_general x1 -> x8, matrix products: 2.69 us -> 9.74 us  [on_device(): jnp.einsum('rhc,tc->rht', own_block, prefix_cache, preferred_element_type...]
    all_to_all x1, blocking collectives: 11.8 us -> 8.85 us  [on_device(): lax.all_to_all(by_owner(row_mass), 'ctx', split_axis=0, concat_axis=0, ti...]
    ppermute x0 -> x7, starting transfers between devices: none -> 2.98 us  [on_each_block(): lax.ppermute(shard, axis, [(d, (d + 1) % ways) for d in range(ways)])]
    reduce_max x0 -> x1, other arithmetic: none -> 1.84 us  [partial_stats(): row_peak = jnp.max(jnp.where(visible, scores, masked_value), axis=2)]
  transfers between devices with their start and end apart: 2 -> 9, of which waited for: 2 -> 9; matrix products, arithmetic and copies ran while one was open for 5% -> 6% of each run, Pallas kernels for 0% -> 0%
where the time goes in v1:
time: 152 us
  waiting for transfers between devices  52.7 us (35%)
  blocking collectives  49.7 us (33%)
  matrix products  26.4 us (17%)
  starting transfers between devices  11.4 us (8%)
  other arithmetic  6.28 us (4%)
  local copies, waits for them, and re-layouts  3.7 us (2%)
  between operations  1.53 us (1%)
    ppermute x7, waiting for transfers between devices, on_each_block(): lax.ppermute(shard, axis, [(d, (d + 1) % ways) for d in range(ways)])  43.9 us
    all_gather x1, blocking collectives, on_device(): every_value = lax.all_gather(flat_values, 'ctx', axis=0, tiled=True)  30.6 us
    unnamed x1, blocking collectives  10.3 us
    dot_general x8, matrix products, on_device(): jnp.einsum('rhc,tc->rht', own_block, prefix_cache, preferred_element_type...  9.74 us
    all_to_all x1, blocking collectives, on_device(): lax.all_to_all(by_owner(row_mass), 'ctx', split_axis=0, concat_axis=0, ti...  8.85 us
    all_to_all x1, waiting for transfers between devices, on_device(): lax.all_to_all(by_owner(row_weighted), 'ctx', split_axis=0, concat_axis=0...  8 us
    dot_general x2, matrix products, partial_stats(): jnp.einsum(pattern, weights, values, preferred_element_type=jnp.float32)  5.87 us
    all_to_all x1, starting transfers between devices, on_device(): lax.all_to_all(by_owner(row_weighted), 'ctx', split_axis=0, concat_axis=0...  5.17 us
  transfers between devices with their start and end apart: 9, of which 9 were waited for; matrix products, arithmetic and copies ran while one was open for 6% of the time, Pallas kernels for 0%

profile of v1, /device:TPU:0, one launch (start us, length us, event | category | flops | bytes accessed | tf_op | source)
XLA Modules:
  0.0 151.6 jit_solution(12705724135464203755)
XLA Ops:
  0.0 0.0 copy-start
  0.0 0.7 copy-done
  0.7 2.8 %fusion.27 = bf16[32,1,512]{2,1,0:T(2,128)(2,1)S(1)} fusion(bf16[32,128,512]{2,1,0:T(8,128)(2,1)} %param.12, bf16[32,128,1]{1,0,2:T(8,128)(2,1)S(1)} %bitcast.112), kind=kOutput, calls=%fused_computation.63 | convolution fusion | flops 4194304 | bytes 4235264 | tf_op jit(solution)/shard_map/rhn,hnc->rhc/dot_general | solution.py:53
  3.6 0.7 pad_maximum_fusion
  4.3 3.0 %collective-permute-start = (bf16[1,32,576]{2,1,0:T(8,128)(2,1)S(1)}, bf16[1,32,576]{2,1,0:T(8,128)(2,1)S(1)}, u32[]{:S(2)}, u32[]{:S(2)}) collective-permute-start(bf16[1,32,576]{2,1,0:T(8,128)(2,1)S(1)} %pad_maximum_fusion), channel_id=1, source_target_pairs={{0,4},{4,8},{8,12},{12,16},{16,20},{20,24},{24,28},{28,0},{1,5},{5... | collective-permute-start | bytes 110600 | tf_op jit(solution)/shard_map/ppermute | solution.py:18
  7.2 5.0 %collective-permute-done = bf16[1,32,576]{2,1,0:T(8,128)(2,1)S(1)} collective-permute-done((bf16[1,32,576]{2,1,0:T(8,128)(2,1)S(1)}, bf16[1,32,576]{2,1,0:T(8,128)(2,1)S(1)}, u32[]{:S(2)}, u32[]{:S(2)}) %collective-permute-start) | collective-permute-done | bytes 36896 | tf_op jit(solution)/shard_map/ppermute | solution.py:18
  12.2 0.0 collective-permute-start.1
  12.2 6.7 %collective-permute-done.1 = bf16[1,32,576]{2,1,0:T(8,128)(2,1)S(1)} collective-permute-done((bf16[1,32,576]{2,1,0:T(8,128)(2,1)S(1)}, bf16[1,32,576]{2,1,0:T(8,128)(2,1)S(1)}, u32[]{:S(2)}, u32[]{:S(2)}) %collective-permute-start.1) | collective-permute-done | bytes 36896 | tf_op jit(solution)/shard_map/ppermute | solution.py:18
  18.9 0.0 collective-permute-start.2
  18.9 6.7 %collective-permute-done.2 = bf16[1,32,576]{2,1,0:T(8,128)(2,1)S(1)} collective-permute-done((bf16[1,32,576]{2,1,0:T(8,128)(2,1)S(1)}, bf16[1,32,576]{2,1,0:T(8,128)(2,1)S(1)}, u32[]{:S(2)}, u32[]{:S(2)}) %collective-permute-start.2) | collective-permute-done | bytes 36896 | tf_op jit(solution)/shard_map/ppermute | solution.py:18
  25.6 0.0 collective-permute-start.3
  25.6 6.7 %collective-permute-done.3 = bf16[1,32,576]{2,1,0:T(8,128)(2,1)S(1)} collective-permute-done((bf16[1,32,576]{2,1,0:T(8,128)(2,1)S(1)}, bf16[1,32,576]{2,1,0:T(8,128)(2,1)S(1)}, u32[]{:S(2)}, u32[]{:S(2)}) %collective-permute-start.3) | collective-permute-done | bytes 36896 | tf_op jit(solution)/shard_map/ppermute | solution.py:18
  32.3 0.0 collective-permute-start.4
  32.3 0.7 broadcast_multiply_fusion
  33.0 6.4 %collective-permute-done.4 = bf16[1,32,576]{2,1,0:T(8,128)(2,1)S(1)} collective-permute-done((bf16[1,32,576]{2,1,0:T(8,128)(2,1)S(1)}, bf16[1,32,576]{2,1,0:T(8,128)(2,1)S(1)}, u32[]{:S(2)}, u32[]{:S(2)}) %collective-permute-start.4) | collective-permute-done | bytes 36896 | tf_op jit(solution)/shard_map/ppermute | solution.py:18
  39.4 0.0 collective-permute-start.5
  39.4 0.1 iota_add_fusion
  39.5 0.1 add.51
  39.5 6.5 %collective-permute-done.5 = bf16[1,32,576]{2,1,0:T(8,128)(2,1)S(1)} collective-permute-done((bf16[1,32,576]{2,1,0:T(8,128)(2,1)S(1)}, bf16[1,32,576]{2,1,0:T(8,128)(2,1)S(1)}, u32[]{:S(2)}, u32[]{:S(2)}) %collective-permute-start.5) | collective-permute-done | bytes 36896 | tf_op jit(solution)/shard_map/ppermute | solution.py:18
  46.1 0.0 collective-permute-start.6
  46.1 0.7 broadcast_compare_fusion
  46.9 0.0 copy-start.1
  46.9 5.9 %collective-permute-done.6 = bf16[1,32,576]{2,1,0:T(8,128)(2,1)S(1)} collective-permute-done((bf16[1,32,576]{2,1,0:T(8,128)(2,1)S(1)}, bf16[1,32,576]{2,1,0:T(8,128)(2,1)S(1)}, u32[]{:S(2)}, u32[]{:S(2)}) %collective-permute-start.6) | collective-permute-done | bytes 36896 | tf_op jit(solution)/shard_map/ppermute | solution.py:18
  52.8 3.2 %constant_dynamic-update-slice_fusion.15 = (f32[16,32,4096]{2,1,0:T(8,128)S(1)}, f32[1,32,4096]{2,1,0:T(8,128)S(1)}) fusion(bf16[4096,576]{0,1:T(8,128)(2,1)} %param.15, bf16[1,32,576]{2,1,0:T(8,128)(2,1)S(1)} %collective-permute-done.6), kind=kOutput, calls=%fused_computation.57 | convolution fusion | flops 150994944 | bytes 5804032 | tf_op jit(solution)/shard_map/rhc,tc->rht/dot_general | solution.py:69
  56.0 0.0 copy-done.1
  56.0 0.9 constant_dynamic-update-slice_fusion.14
  57.0 0.9 constant_dynamic-update-slice_fusion.13
  57.9 0.9 constant_dynamic-update-slice_fusion.12
  58.8 0.9 constant_dynamic-update-slice_fusion.11
  59.8 0.0 copy-start.4
  59.8 0.9 constant_dynamic-update-slice_fusion.10
  60.7 0.9 constant_dynamic-update-slice_fusion.9
  61.6 0.0 copy-done.4
  61.7 0.9 constant_dynamic-update-slice_fusion.8
  62.6 0.1 constant_dynamic-update-slice_fusion.7
  62.9 0.0 copy-start.2
  63.0 1.8 %select_reduce_fusion = f32[8,32]{1,0:T(8,128)} fusion(f32[16,32,4096]{2,1,0:T(8,128)S(1)} %constant_dynamic-update-slice_fusion, s32[]{:T(128)S(6)} %select_n.30, pred[8,4096]{1,0:T(8,128)(4,1)S(1)} %broadcast_compare_fusion), kind=kLoop, calls=%fused_computation.13 | loop fusion | flops 3145472 | bytes 4228100 | tf_op jit(solution)/shard_map/reduce_max | solution.py:29
  64.8 1.4 copy-done.2
  66.2 1.9 %convert_reduce_fusion = f32[8,32]{1,0:T(8,128)S(1)} fusion(f32[8,32]{1,0:T(8,128)} %select_reduce_fusion, f32[16,32,4096]{2,1,0:T(8,128)S(1)} %constant_dynamic-update-slice_fusion, s32[]{:T(128)S(6)} %select_n.30, pred[8,4096]{1,0:T(8,128)(4,1)S(1)} %broadcast_compare_fusion), kind=kLoop, calls=%fused_computation.10 | loop fusion | flops 6291200 | bytes 4229124 | tf_op jit(solution)/shard_map/reduce_sum | solution.py:31
  68.0 8.8 %all_to_all.15 = f32[8,1,32]{2,1,0:T(1,128)S(1)} all-to-all(f32[8,1,32]{2,1,0:T(1,128)S(1)} %bitcast.118), channel_id=1, replica_groups=mesh['ctx'=8,'tp'=4] {'ctx'}, dimensions={0} | all-to-all | bytes 2048 | tf_op jit(solution)/shard_map/all_to_all | solution.py:94
  76.9 3.2 %all-to-all-start = ((f32[8,1,32]{2,1,0:T(1,128)}), f32[8,1,32]{2,1,0:T(1,128)S(1)}, u32[]{:S(2)}, u32[]{:S(2)}) async-start(f32[8,1,32]{2,1,0:T(1,128)} %bitcast.20), calls=%async_computation | async-start | bytes 8192 | tf_op jit(solution)/shard_map/all_to_all | solution.py:93
  80.1 0.0 copy-start.5
  80.1 0.0 copy-start.3
  80.1 5.7 %fusion.3 = f32[8,1,32,512]{3,2,1,0:T(8,128)} fusion(bf16[4096,576]{0,1:T(8,128)(2,1)} %param.15, f32[16,32,4096]{2,1,0:T(8,128)} %copy-done.2, s32[]{:T(128)S(6)} %select_n.30, f32[8,32]{1,0:T(8,128)} %select_reduce_fusion, pred[8,4096]{1,0:T(8,128)(4,1)S(1)} %broadcast_compare_fusion), kind=kOutput, calls=%fused_computation.15 | convolution fusion | flops 1077936128 | bytes 8949764 | tf_op jit(solution)/shard_map/rht,tc->rhc/dot_general | solution.py:32
  85.8 0.7 all-to-all-done
  86.6 5.2 %all-to-all-start.1 = ((f32[8,1,32,512]{3,2,1,0:T(8,128)}), f32[8,1,32,512]{3,2,1,0:T(8,128)S(1)}, u32[]{:S(2)}, u32[]{:S(2)}) async-start(f32[8,1,32,512]{3,2,1,0:T(8,128)} %fusion.3), calls=%async_computation.1 | async-start | bytes 1048576 | tf_op jit(solution)/shard_map/all_to_all | solution.py:95
  92.4 0.0 copy-done.5
  92.4 0.6 dynamic-slice
  93.6 0.0 copy-done.3
  93.6 0.3 select_reduce_fusion.1
  93.9 0.2 convert_reduce_fusion.1
  94.2 8.0 %all-to-all-done.1 = f32[8,1,32,512]{3,2,1,0:T(8,128)S(1)} async-done(((f32[8,1,32,512]{3,2,1,0:T(8,128)}), f32[8,1,32,512]{3,2,1,0:T(8,128)S(1)}, u32[]{:S(2)}, u32[]{:S(2)}) %all-to-all-start.1) | async-done | bytes 524320 | tf_op jit(solution)/shard_map/all_to_all | solution.py:95
  102.2 0.1 multiply_reduce_fusion
  102.3 0.2 fusion.8
  102.5 3.5 %fusion.15 = f32[32,1,128]{2,1,0:T(1,128)S(1)} fusion(bf16[32,512,128]{2,1,0:T(8,128)(2,1)} %param.13, f32[32,512,1]{1,0,2:T(8,128)S(1)} %fusion.8), kind=kOutput, calls=%fused_computation.29 | convolution fusion | flops 25165824 | bytes 4276224 | tf_op jit(solution)/shard_map/rhc,hcv->rhv/dot_general | solution.py:37
  106.0 30.6 %all-gather = bf16[8,1,4096]{2,1,0:T(2,128)(2,1)S(1)} all-gather(bf16[1,1,4096]{2,1,0:T(2,128)(2,1)S(1)} %reshape.203), channel_id=1, replica_groups=mesh['ctx'=8,'tp'=4] {'ctx'}, dimensions={0}, use_global_device_ids=true | all-gather | bytes 73728 | tf_op jit(solution)/shard_map/all_gather | solution.py:108
  136.6 4.1 %fusion.12 = f32[8,896]{1,0:T(8,128)S(1)} fusion(bf16[4096,896]{1,0:T(8,128)(2,1)} %param.14, bf16[8,1,4096]{2,1,0:T(2,128)(2,1)S(1)} %all-gather), kind=kOutput, calls=%fused_computation.25 | convolution fusion | flops 58720256 | bytes 7434240 | tf_op jit(solution)/shard_map/dot_general | solution.py:110
  140.7 10.3 %all-reduce = bf16[8,896]{1,0:T(8,128)(2,1)S(1)} all-reduce(f32[8,896]{1,0:T(8,128)S(1)} %fusion.12), channel_id=2, replica_groups=mesh['ctx'=8,'tp'=4] {'tp'}, use_global_device_ids=true, to_apply=%region_7.8.clone | all-reduce | flops 7168 | bytes 43008
  151.1 0.6 dynamic-slice_convert_fusion
  (15 shorter events, 0.4 us)
Async XLA Ops:
  0.0 0.7 copy-start
  4.3 8.0 %collective-permute-start = (bf16[1,32,576]{2,1,0:T(8,128)(2,1)S(1)}, bf16[1,32,576]{2,1,0:T(8,128)(2,1)S(1)}, u32[]{:S(2)}, u32[]{:S(2)}) collective-permute-start(bf16[1,32,576]{2,1,0:T(8,128)(2,1)S(1)} %pad_maximum_fusion), channel_id=1, source_target_pairs={{0,4},{4,8},{8,12},{12,16},{16,20},{20,24},{24,28},{28,0},{1,5},{5... | collective-permute-start | bytes 110600 | tf_op jit(solution)/shard_map/ppermute | solution.py:18
  12.2 6.7 %collective-permute-start.1 = (bf16[1,32,576]{2,1,0:T(8,128)(2,1)S(1)}, bf16[1,32,576]{2,1,0:T(8,128)(2,1)S(1)}, u32[]{:S(2)}, u32[]{:S(2)}) collective-permute-start(bf16[1,32,576]{2,1,0:T(8,128)(2,1)S(1)} %collective-permute-done), channel_id=1, source_target_pairs={{0,4},{4,8},{8,12},{12,16},{16,20},{20,24},{24,28},{28,0},{1,5},{5... | collective-permute-start | bytes 110600 | tf_op jit(solution)/shard_map/ppermute | solution.py:18
  18.9 6.7 %collective-permute-start.2 = (bf16[1,32,576]{2,1,0:T(8,128)(2,1)S(1)}, bf16[1,32,576]{2,1,0:T(8,128)(2,1)S(1)}, u32[]{:S(2)}, u32[]{:S(2)}) collective-permute-start(bf16[1,32,576]{2,1,0:T(8,128)(2,1)S(1)} %collective-permute-done.1), channel_id=1, source_target_pairs={{0,4},{4,8},{8,12},{12,16},{16,20},{20,24},{24,28},{28,0},{1,5},{5... | collective-permute-start | bytes 110600 | tf_op jit(solution)/shard_map/ppermute | solution.py:18
  25.6 6.7 %collective-permute-start.3 = (bf16[1,32,576]{2,1,0:T(8,128)(2,1)S(1)}, bf16[1,32,576]{2,1,0:T(8,128)(2,1)S(1)}, u32[]{:S(2)}, u32[]{:S(2)}) collective-permute-start(bf16[1,32,576]{2,1,0:T(8,128)(2,1)S(1)} %collective-permute-done.2), channel_id=1, source_target_pairs={{0,4},{4,8},{8,12},{12,16},{16,20},{20,24},{24,28},{28,0},{1,5},{5... | collective-permute-start | bytes 110600 | tf_op jit(solution)/shard_map/ppermute | solution.py:18
  32.3 7.0 %collective-permute-start.4 = (bf16[1,32,576]{2,1,0:T(8,128)(2,1)S(1)}, bf16[1,32,576]{2,1,0:T(8,128)(2,1)S(1)}, u32[]{:S(2)}, u32[]{:S(2)}) collective-permute-start(bf16[1,32,576]{2,1,0:T(8,128)(2,1)S(1)} %collective-permute-done.3), channel_id=1, source_target_pairs={{0,4},{4,8},{8,12},{12,16},{16,20},{20,24},{24,28},{28,0},{1,5},{5... | collective-permute-start | bytes 110600 | tf_op jit(solution)/shard_map/ppermute | solution.py:18
  39.4 6.7 %collective-permute-start.5 = (bf16[1,32,576]{2,1,0:T(8,128)(2,1)S(1)}, bf16[1,32,576]{2,1,0:T(8,128)(2,1)S(1)}, u32[]{:S(2)}, u32[]{:S(2)}) collective-permute-start(bf16[1,32,576]{2,1,0:T(8,128)(2,1)S(1)} %collective-permute-done.4), channel_id=1, source_target_pairs={{0,4},{4,8},{8,12},{12,16},{16,20},{20,24},{24,28},{28,0},{1,5},{5... | collective-permute-start | bytes 110600 | tf_op jit(solution)/shard_map/ppermute | solution.py:18
  46.1 6.7 %collective-permute-start.6 = (bf16[1,32,576]{2,1,0:T(8,128)(2,1)S(1)}, bf16[1,32,576]{2,1,0:T(8,128)(2,1)S(1)}, u32[]{:S(2)}, u32[]{:S(2)}) collective-permute-start(bf16[1,32,576]{2,1,0:T(8,128)(2,1)S(1)} %collective-permute-done.5), channel_id=1, source_target_pairs={{0,4},{4,8},{8,12},{12,16},{16,20},{20,24},{24,28},{28,0},{1,5},{5... | collective-permute-start | bytes 110600 | tf_op jit(solution)/shard_map/ppermute | solution.py:18
  46.9 9.2 %copy-start.1 = (bf16[4096,576]{0,1:T(8,128)(2,1)S(1)}, bf16[4096,576]{0,1:T(8,128)(2,1)}, u32[]{:S(2)}) copy-start(bf16[4096,576]{0,1:T(8,128)(2,1)} %param.15) | copy-start | bytes 14155780
  59.8 1.9 %copy-start.4 = (bf16[1,32,64]{2,1,0:T(8,128)(2,1)S(1)}, bf16[1,32,64]{2,1,0:T(8,128)(2,1)}, u32[]{:S(2)}) copy-start(bf16[1,32,64]{2,1,0:T(8,128)(2,1)} %param.11) | copy-start | bytes 12292
  62.9 3.2 %copy-start.2 = (f32[16,32,4096]{2,1,0:T(8,128)}, f32[16,32,4096]{2,1,0:T(8,128)S(1)}, u32[]{:S(2)}) copy-start(f32[16,32,4096]{2,1,0:T(8,128)S(1)} %constant_dynamic-update-slice_fusion) | copy-start | bytes 25165828
  76.9 9.7 %all-to-all-start = ((f32[8,1,32]{2,1,0:T(1,128)}), f32[8,1,32]{2,1,0:T(1,128)S(1)}, u32[]{:S(2)}, u32[]{:S(2)}) async-start(f32[8,1,32]{2,1,0:T(1,128)} %bitcast.20), calls=%async_computation | async-start | bytes 8192 | tf_op jit(solution)/shard_map/all_to_all | solution.py:93
  80.1 12.3 %copy-start.5 = (u32[32]{0:T(128)S(1)}, u32[32]{0:T(128)}, u32[]{:S(2)}) copy-start(u32[32]{0:T(128)} %constant.47) | copy-start | bytes 388
  80.1 13.5 %copy-start.3 = (bf16[1,256,576]{1,2,0:T(8,128)(2,1)S(1)}, bf16[1,256,576]{1,2,0:T(8,128)(2,1)}, u32[]{:S(2)}) copy-start(bf16[1,256,576]{1,2,0:T(8,128)(2,1)} %param.18) | copy-start | bytes 884740
  86.6 15.6 %all-to-all-start.1 = ((f32[8,1,32,512]{3,2,1,0:T(8,128)}), f32[8,1,32,512]{3,2,1,0:T(8,128)S(1)}, u32[]{:S(2)}, u32[]{:S(2)}) async-start(f32[8,1,32,512]{3,2,1,0:T(8,128)} %fusion.3), calls=%async_computation.1 | async-start | bytes 1048576 | tf_op jit(solution)/shard_map/all_to_all | solution.py:95
